TPU v7x, 32 devices: a whole 2x2x4 slice. The times are simulated.
32 devices in a mesh: groups: 2 (over y), st: 4 (over x, core), ch: 4 (over z).
Axes of the slice: x: 2, y: 2, z: 4, core: 2. Of those that a mesh axis runs over, the one named last changes fastest.
Arguments:
- latents: bfloat16 [1280, 1024], P('ch', ('groups', 'st')), parts along dimension 1, may hold values from -6 to 6
- spatial_weight: bfloat16 [9, 1280, 1280], P(None, 'ch'), may hold values from -0.0546875 to 0.0546875
- temporal_weight: bfloat16 [3, 1280, 1280], P(None, 'ch'), may hold values from -0.09375 to 0.09375
- cotangent: bfloat16 [1280, 1024], P('ch', ('groups', 'st')), parts along dimension 1, may hold values from -6 to 6
Outputs:
- temporal_out: bfloat16 [1280, 1024], P('ch', ('groups', 'st')), parts along dimension 1
- latent_grad: bfloat16 [1280, 1024], P('ch', ('groups', 'st')), parts along dimension 1
- spatial_grad: float32 [18, 1280, 1280], P('groups', 'ch', 'st'), parts along dimension 0
- temporal_grad: float32 [6, 1280, 1280], P('groups', 'ch', 'st'), parts along dimension 0
There are 2 independent parts, one for each index of `groups`. A program takes and returns all parts, laid end to end along the dimension named above; an argument that names none is the same for every part. Nothing has to cross between parts.
All inputs are finite; a program needn't handle non-finite values.
Results may differ from a plain program's by a relative error of at most 0.008.
Values may be sent and summed in bfloat16 or wider, within the bound.
No kernel may reach another device: no remote copies, remote signals or barrier semaphores. Data moves between devices by JAX's collectives and lax.ppermute only.
A program may use at most 192 MiB of HBM per device.

v0:
```python
import math
import jax
import jax.numpy as jnp
from jax import lax
from jax.sharding import PartitionSpec as P

FT = 2
RT = 2
W = 32
RBANDS = 2
spatial_offsets = tuple(
    ((row_step, col_step) for row_step in (-1, 0, 1) for col_step in (-1, 0, 1))
)
frame_offsets = (-1, 0, 1)


def passed_along(shard, axis, by):
    devices = lax.axis_size(axis)
    pairs = [(i, i + by) for i in range(devices) if 0 <= i + by < devices]
    return lax.ppermute(shard, axis, pairs)


def neighbour(slab, distance):
    return passed_along(slab, "st", distance)


def circulate(data, fold, initial):
    return fold(initial, lax.all_gather(data, "ch", axis=0, tiled=True), jnp.int32(0))


def regather(data, build):
    return build(lax.all_gather(data, "ch", axis=0, tiled=True), jnp.int32(0))


def pad_rows(field):
    channels = field.shape[0]
    layered = field.reshape(channels, FT, RT * W)
    band = lax.axis_index("st") % RBANDS
    upper = neighbour(layered[:, :, (RT - 1) * W :], 1)
    lower = neighbour(layered[:, :, :W], -1)
    upper = jnp.where(band > 0, upper, jnp.zeros_like(upper))
    lower = jnp.where(band < RBANDS - 1, lower, jnp.zeros_like(lower))
    margin = jnp.zeros((channels, FT, 1), field.dtype)
    return jnp.concatenate([margin, upper, layered, lower, margin], axis=2)


def spatial_piece(padded, row_step, col_step):
    first_cell = 1 + (1 + row_step) * W + col_step
    window = lax.slice_in_dim(padded, first_cell, first_cell + RT * W, axis=2)
    column = jnp.arange(RT * W, dtype=jnp.int32) % W + col_step
    inside = (column >= 0) & (column < W)
    window = jnp.where(inside, window, jnp.zeros_like(window))
    return window.reshape(padded.shape[0], FT * RT * W)


def pad_frames(field):
    frame_cells = RT * W
    earlier = neighbour(field[:, (FT - 1) * frame_cells :], RBANDS)
    following = neighbour(field[:, :frame_cells], -RBANDS)
    return jnp.concatenate([earlier, field, following], axis=1)


def frame_piece(padded, frame_step):
    frame_cells = RT * W
    first_cell = (1 + frame_step) * frame_cells
    return lax.slice_in_dim(padded, first_cell, first_cell + FT * frame_cells, axis=1)


def contract(weights, pieces):
    running = jnp.dot(weights[0], pieces[0], preferred_element_type=jnp.float32)
    for position in range(1, len(pieces)):
        running = running + jnp.dot(
            weights[position], pieces[position], preferred_element_type=jnp.float32
        )
    return running


def outer_sums(gradient, pieces):
    contraction = (((1,), (1,)), ((), ()))
    return jnp.stack(
        [
            lax.dot_general(gradient, tap_piece, contraction, preferred_element_type=jnp.float32)
            for tap_piece in pieces
        ]
    )


def on_device(latents, spatial_weight, temporal_weight, cotangent):
    channels, tile_cells = latents.shape
    grad_scale = 1.0 / math.sqrt(tile_cells * lax.axis_size("st"))
    spatial_back, temporal_back = (
        lax.all_to_all(
            jnp.transpose(spatial_weight, (0, 2, 1)), "ch", split_axis=1, concat_axis=2, tiled=True
        ),
        lax.all_to_all(
            jnp.transpose(temporal_weight, (0, 2, 1)), "ch", split_axis=1, concat_axis=2, tiled=True
        ),
    )
    empty_sum = jnp.zeros((channels, tile_cells), jnp.float32)
    latent_pad = pad_rows(latents)
    latent_store = jnp.zeros((1,), jnp.bfloat16)

    def spatial_forward(carry, portion, offset):
        running, stored = carry
        running = contract(
            spatial_weight,
            [spatial_piece(portion, row_step, col_step) for row_step, col_step in spatial_offsets],
        )
        return (running, stored)

    spatial_sum, latent_store = circulate(latent_pad, spatial_forward, (empty_sum, latent_store))
    hidden = (latents.astype(jnp.float32) + spatial_sum).astype(jnp.bfloat16)
    hidden_pad = pad_frames(hidden)
    hidden_store = jnp.zeros((1,), jnp.bfloat16)

    def temporal_forward(carry, portion, offset):
        running, stored = carry
        running = contract(
            temporal_weight, [frame_piece(portion, frame_step) for frame_step in frame_offsets]
        )
        return (running, stored)

    temporal_sum, hidden_store = circulate(hidden_pad, temporal_forward, (empty_sum, hidden_store))
    temporal_out = (hidden.astype(jnp.float32) + temporal_sum).astype(jnp.bfloat16)
    upstream_pad = pad_frames(cotangent)

    def temporal_backward(running, portion, offset):
        return contract(
            temporal_back, [frame_piece(portion, -frame_step) for frame_step in frame_offsets]
        )

    hidden_back = circulate(upstream_pad, temporal_backward, empty_sum)

    def temporal_terms(portion, offset):
        return outer_sums(
            cotangent, [frame_piece(portion, frame_step) for frame_step in frame_offsets]
        )

    temporal_grads = regather(hidden_pad, temporal_terms)
    hidden_grad = (cotangent.astype(jnp.float32) + hidden_back).astype(jnp.bfloat16)
    grad_pad = pad_rows(hidden_grad)

    def spatial_backward(running, portion, offset):
        return contract(
            spatial_back,
            [
                spatial_piece(portion, -row_step, -col_step)
                for row_step, col_step in spatial_offsets
            ],
        )

    latent_back = circulate(grad_pad, spatial_backward, empty_sum)

    def spatial_terms(portion, offset):
        return outer_sums(
            hidden_grad,
            [spatial_piece(portion, row_step, col_step) for row_step, col_step in spatial_offsets],
        )

    spatial_grads = regather(latent_pad, spatial_terms)
    latent_grad = (hidden_grad.astype(jnp.float32) + latent_back).astype(jnp.bfloat16)
    spatial_total, temporal_total = (
        lax.psum_scatter(
            spatial_grads.astype(jnp.bfloat16), "st", scatter_dimension=2, tiled=True
        ).astype(jnp.float32),
        lax.psum_scatter(
            temporal_grads.astype(jnp.bfloat16), "st", scatter_dimension=2, tiled=True
        ).astype(jnp.float32),
    )
    return (temporal_out, latent_grad, spatial_total * grad_scale, temporal_total * grad_scale)


def solution(mesh):
    return jax.shard_map(
        on_device,
        mesh=mesh,
        in_specs=(
            P("ch", ("groups", "st")),
            P(None, "ch", None),
            P(None, "ch", None),
            P("ch", ("groups", "st")),
        ),
        out_specs=(
            P("ch", ("groups", "st")),
            P("ch", ("groups", "st")),
            P("groups", "ch", "st"),
            P("groups", "ch", "st"),
        ),
        check_vma=False,
    )
```

profile of v0, /device:TPU:0, one launch (start us, length us, event | category | flops | bytes accessed | tf_op | source)
XLA Modules:
  0.0 648.7 jit_solution(954349262117856633)
XLA Ops:
  7.2 7.7 %copy.23 = bf16[3,320,1280]{1,0,2:T(4,128)(2,1)} copy(bf16[3,320,1280]{2,1,0:T(8,128)(2,1)} %param.6) | data formatting | bytes 4915200 | tf_op args[2]
  14.9 6.3 all-to-all-start
  22.6 4.6 collective-permute-start.4
  30.0 1.7 collective-permute-done.1
  33.0 87.4 %all_gather.16 = bf16[1280,256]{1,0:T(8,128)(2,1)S(1)} all-gather(bf16[320,256]{1,0:T(8,128)(2,1)S(1)} %pad_maximum_fusion.2), channel_id=1, replica_groups=mesh['groups'=2,'st'=4,'ch'=4] {'ch'}, dimensions={0}, use_global_device_ids=true | all-gather | bytes 819200 | tf_op jit(solution)/shard_map/all_gather | solution.py:28
  120.4 24.1 %all_gather.14 = bf16[1280,2,130]{2,1,0:T(2,128)(2,1)S(1)} all-gather(bf16[320,2,130]{2,1,0:T(2,128)(2,1)S(1)} %copy.13), channel_id=1, replica_groups=mesh['groups'=2,'st'=4,'ch'=4] {'ch'}, dimensions={0}, use_global_device_ids=true | all-gather | bytes 832000 | tf_op jit(solution)/shard_map/all_gather | solution.py:28
  144.4 4.9 copy.63
  149.3 2.3 fusion.70
  151.6 2.8 squeeze.85
  154.4 2.8 squeeze.84
  157.1 1.7 squeeze.86
  158.8 1.6 fusion.60
  160.4 1.5 convolution_add_fusion.1
  161.9 1.5 fusion.29
  165.1 6.9 %fusion.72 = (bf16[1280,2,64]{2,1,0:T(2,128)(2,1)S(1)}, bf16[1280,2,64]{2,1,0:T(2,128)(2,1)}, bf16[1280,2,64]{2,1,0:T(2,128)(2,1)}, bf16[1280,2,64]{2,1,0:T(2,12...) fusion(bf16[1280,2,130]{2,1,0:T(2,128)(2,1)S(1)} %all_gather.14), kind=kLoop, calls=%fused_computation.137 | loop fusion | bytes 5898240 | tf_op jit(solution)/shard_map/slice | solution.py:49
  172.1 2.0 copy.45
  174.1 2.0 copy.48
  176.1 2.0 copy.42
  178.1 2.0 copy.46
  180.1 2.0 copy.49
  182.2 2.0 copy.43
  184.2 2.0 copy.47
  189.7 3.7 collective-permute-done.7
  194.4 24.4 %all_gather.17 = bf16[1280,2,130]{2,1,0:T(2,128)(2,1)S(1)} all-gather(bf16[320,2,130]{2,1,0:T(2,128)(2,1)S(1)} %copy.26), channel_id=1, replica_groups=mesh['groups'=2,'st'=4,'ch'=4] {'ch'}, dimensions={0}, use_global_device_ids=true | all-gather | bytes 832000 | tf_op jit(solution)/shard_map/all_gather | solution.py:28
  218.8 6.9 %fusion.71 = (bf16[1280,2,64]{2,1,0:T(2,128)(2,1)S(1)}, bf16[1280,2,64]{2,1,0:T(2,128)(2,1)}, bf16[1280,2,64]{2,1,0:T(2,128)(2,1)}, bf16[1280,2,64]{2,1,0:T(2,12...) fusion(bf16[1280,2,130]{2,1,0:T(2,128)(2,1)S(1)} %all_gather.17), kind=kLoop, calls=%fused_computation.136 | loop fusion | bytes 5898240 | tf_op jit(solution)/shard_map/slice | solution.py:49
  229.0 2.2 copy.58
  231.2 2.0 copy.52
  233.2 2.0 copy.55
  235.2 2.0 copy.57
  237.2 2.0 copy.51
  239.2 2.0 copy.54
  241.3 2.7 broadcast_select_fusion.12
  246.2 2.5 broadcast_select_fusion.6
  254.5 4.6 collective-permute-start.2
  259.5 1.6 collective-permute-done.2
  261.2 17.7 %all_gather.15 = bf16[1280,256]{1,0:T(8,128)(2,1)S(1)} all-gather(bf16[320,256]{1,0:T(8,128)(2,1)S(1)} %pad_maximum_fusion.1), channel_id=1, replica_groups=mesh['groups'=2,'st'=4,'ch'=4] {'ch'}, dimensions={0}, use_global_device_ids=true | all-gather | bytes 819200 | tf_op jit(solution)/shard_map/all_gather | solution.py:28
  280.4 6.0 copy.40
  286.5 8.3 %reshape.123 = bf16[1280,960]{1,0:T(8,128)(2,1)} reshape(bf16[1280,3,320]{2,1,0:T(4,128)(2,1)} %bitcast.203) | data formatting | bytes 4915200
  294.9 20.9 %copy.28 = bf16[9,320,1280]{1,0,2:T(8,128)(2,1)} copy(bf16[9,320,1280]{2,1,0:T(8,128)(2,1)} %param.5) | data formatting | bytes 14745600 | tf_op args[1]
  327.3 20.2 %copy.38 = bf16[9,320,1280]{1,0,2:T(8,128)(2,1)} copy(bf16[9,320,1280]{2,1,0:T(8,128)(2,1)} %fusion.17) | data formatting | bytes 14745600
  347.5 18.7 %reshape.121 = bf16[1280,2880]{1,0:T(8,128)(2,1)} reshape(bf16[1280,9,320]{2,1,0:T(8,128)(2,1)} %bitcast.197) | data formatting | bytes 14745600
  366.3 14.2 %bitcast_bitcast_fusion = bf16[1280,9,320]{2,1,0:T(8,128)(2,1)} fusion(bf16[9,320,1280]{1,0,2:T(8,128)(2,1)} %copy.28), kind=kLoop, calls=%fused_computation.142 | loop fusion | bytes 14745600
  380.5 15.3 %reshape.125 = bf16[4,2,460800]{2,1,0:T(2,128)(2,1)} reshape(bf16[1280,9,320]{2,1,0:T(8,128)(2,1)} %bitcast_bitcast_fusion) | data formatting | bytes 14745600
  395.8 6.0 all-to-all-start.1
  403.7 2.5 reshape.124
  408.6 152.6 %all-to-all-done.1 = bf16[4,2,460800]{2,1,0:T(2,128)(2,1)} async-done(((bf16[4,2,460800]{2,1,0:T(2,128)(2,1)}), bf16[4,2,460800]{2,1,0:T(2,128)(2,1)}, u32[]{:S(2)}, u32[]{:S(2)}) %all-to-all-start.1) | async-done | bytes 7372832 | tf_op jit(solution)/shard_map/all_to_all | solution.py:92
  561.2 16.0 %reshape.126 = bf16[1280,9,320]{2,1,0:T(8,128)(2,1)} reshape(bf16[4,2,460800]{2,1,0:T(2,128)(2,1)} %all-to-all-done.1) | data formatting | bytes 14745600
  577.1 12.7 %copy.62 = bf16[9,4,320,320]{3,1,2,0:T(4,128)(2,1)S(1)} copy(bf16[9,4,320,320]{3,0,2,1:T(8,128)(2,1)} %bitcast.198) | data formatting | bytes 14745600 | tf_op jit(solution)/shard_map/all_to_all | solution.py:92
  589.9 4.4 fusion.69
  594.3 2.8 squeeze.87
  597.0 2.8 squeeze.88
  599.8 2.8 squeeze.89
  602.6 2.9 squeeze.90
  605.5 2.8 squeeze.91
  608.2 2.8 squeeze.92
  611.0 1.7 squeeze.93
  614.2 1.7 fusion.77
  616.0 1.6 convolution_add_fusion.11
  617.6 1.6 convolution_add_fusion.10
  619.2 1.6 convolution_add_fusion.9
  620.9 1.6 convolution_add_fusion.8
  627.6 5.6 reshape.122
  633.2 6.0 copy.39
  639.2 2.5 convert_multiply_fusion
  (142 shorter events, 47.3 us)
Async XLA Ops:
  7.2 14.0 %copy-start = (bf16[320,128]{1,0:T(8,128)(2,1)S(1)}, bf16[320,128]{1,0:T(8,128)(2,1)}, u32[]{:S(2)}) copy-start(bf16[320,128]{1,0:T(8,128)(2,1)} %param.7) | copy-start | bytes 245764
  7.2 20.0 %copy-start.29 = (bf16[320,128]{1,0:T(8,128)(2,1)S(1)}, bf16[320,128]{1,0:T(8,128)(2,1)}, u32[]{:S(2)}) copy-start(bf16[320,128]{1,0:T(8,128)(2,1)} %param.4) | copy-start | bytes 245764
  14.9 129.6 %all-to-all-start = ((bf16[3,1280,320]{2,0,1:T(4,128)(2,1)}), bf16[3,1280,320]{2,0,1:T(4,128)(2,1)}, u32[]{:S(2)}, u32[]{:S(2)}) async-start(bf16[3,1280,320]{2,0,1:T(4,128)(2,1)} %bitcast.202), calls=%async_computation | async-start | bytes 7864320 | tf_op jit(solution)/shard_map/all_to_all | solution.py:95
  21.2 382.5 %reduce-scatter.9.cloned.1.call-start = ((), (), s32[]{:S(2)}) async-start(), calls=%async_computation.5 | async-start | bytes 3276800
  21.3 11.5 %collective-permute-start.5 = (bf16[320,64]{1,0:T(8,128)(2,1)S(1)}, bf16[320,64]{1,0:T(8,128)(2,1)S(1)}, u32[]{:S(2)}, u32[]{:S(2)}) collective-permute-start(bf16[320,64]{1,0:T(8,128)(2,1)S(1)} %get-tuple-element.39), channel_id=1, source_target_pairs={{8,0},{12,4},{9,1},{13,5},{10,2},{14,6},{11,3},{15,7},{24,16},{28,... | collective-permute-start | bytes 122888 | tf_op jit(solution)/shard_map/ppermute | solution.py:20
  22.6 10.2 %collective-permute-start.4 = (bf16[320,64]{1,0:T(8,128)(2,1)S(1)}, bf16[320,64]{1,0:T(8,128)(2,1)S(1)}, u32[]{:S(2)}, u32[]{:S(2)}) collective-permute-start(bf16[320,64]{1,0:T(8,128)(2,1)S(1)} %get-tuple-element.38), channel_id=1, source_target_pairs={{0,8},{4,12},{1,9},{5,13},{2,10},{6,14},{3,11},{7,15},{16,24},{20,... | collective-permute-start | bytes 122888 | tf_op jit(solution)/shard_map/ppermute | solution.py:20
  27.3 2.7 collective-permute-start
  28.6 3.1 collective-permute-start.1
  163.6 26.1 %collective-permute-start.6 = (bf16[320,2,32]{0,2,1:T(8,128)(2,1)S(1)}, bf16[320,2,32]{0,2,1:T(8,128)(2,1)S(1)}, u32[]{:S(2)}, u32[]{:S(2)}) collective-permute-start(bf16[320,2,32]{0,2,1:T(8,128)(2,1)S(1)} %get-tuple-element.35), channel_id=1, source_target_pairs={{0,4},{4,8},{8,12},{1,5},{5,9},{9,13},{2,6},{6,10},{10,14},{3,7},{... | collective-permute-start | bytes 122888 | tf_op jit(solution)/shard_map/ppermute | solution.py:20
  188.4 5.0 collective-permute-start.7
  229.0 19.7 %slice-start = ((s8[7372800]{0:T(1024)(128)(4,1)}), s8[3178496]{0:T(1024)(128)(4,1)S(1)}, s32[]{:S(2)}) async-start(s8[7372800]{0:T(1024)(128)(4,1)} %bitcast.200), calls=%async_computation.6 | async-start | bytes 6356992
  241.3 7.5 %slice-start.1 = ((s8[7372800]{0:T(1024)(128)(4,1)}), s8[4194304]{0:T(1024)(128)(4,1)S(1)}, s32[]{:S(2)}) async-start(s8[7372800]{0:T(1024)(128)(4,1)} %bitcast.200), calls=%async_computation.7 | async-start | bytes 8388608
  241.3 7.9 %copy-start.21 = (bf16[1280,2,64]{0,2,1:T(8,128)(2,1)S(1)}, bf16[1280,2,64]{0,2,1:T(8,128)(2,1)}, u32[]{:S(2)}) copy-start(bf16[1280,2,64]{0,2,1:T(8,128)(2,1)} %copy.47) | copy-start | bytes 983044
  241.3 7.9 %copy-start.22 = (bf16[1280,2,64]{0,2,1:T(8,128)(2,1)S(1)}, bf16[1280,2,64]{0,2,1:T(8,128)(2,1)}, u32[]{:S(2)}) copy-start(bf16[1280,2,64]{0,2,1:T(8,128)(2,1)} %copy.50) | copy-start | bytes 983044
  241.3 7.9 %copy-start.23 = (bf16[1280,2,64]{0,2,1:T(8,128)(2,1)S(1)}, bf16[1280,2,64]{0,2,1:T(8,128)(2,1)}, u32[]{:S(2)}) copy-start(bf16[1280,2,64]{0,2,1:T(8,128)(2,1)} %copy.44) | copy-start | bytes 983044
  241.3 7.9 %copy-start.26 = (bf16[1280,2,64]{0,2,1:T(8,128)(2,1)S(1)}, bf16[1280,2,64]{0,2,1:T(8,128)(2,1)}, u32[]{:S(2)}) copy-start(bf16[1280,2,64]{0,2,1:T(8,128)(2,1)} %copy.57) | copy-start | bytes 983044
  241.3 7.9 %copy-start.27 = (bf16[1280,2,64]{0,2,1:T(8,128)(2,1)S(1)}, bf16[1280,2,64]{0,2,1:T(8,128)(2,1)}, u32[]{:S(2)}) copy-start(bf16[1280,2,64]{0,2,1:T(8,128)(2,1)} %copy.51) | copy-start | bytes 983044
  241.3 7.9 %copy-start.28 = (bf16[1280,2,64]{0,2,1:T(8,128)(2,1)S(1)}, bf16[1280,2,64]{0,2,1:T(8,128)(2,1)}, u32[]{:S(2)}) copy-start(bf16[1280,2,64]{0,2,1:T(8,128)(2,1)} %copy.54) | copy-start | bytes 983044
  244.0 0.7 copy-start.19
  244.0 7.5 %copy-start.5 = (bf16[1280,2,64]{0,2,1:T(8,128)(2,1)}, bf16[1280,2,64]{0,2,1:T(8,128)(2,1)S(1)}, u32[]{:S(2)}) copy-start(bf16[1280,2,64]{0,2,1:T(8,128)(2,1)S(1)} %get-tuple-element.43) | copy-start | bytes 983044
  244.0 7.9 %copy-start.3 = (bf16[1280,2,64]{0,2,1:T(8,128)(2,1)}, bf16[1280,2,64]{0,2,1:T(8,128)(2,1)S(1)}, u32[]{:S(2)}) copy-start(bf16[1280,2,64]{0,2,1:T(8,128)(2,1)S(1)} %get-tuple-element.44) | copy-start | bytes 983044
  248.7 4.3 copy-start.7
  248.8 4.3 copy-start.9
  248.8 4.3 copy-start.11
  250.3 29.4 %copy-start.13 = (bf16[1280,2,64]{0,2,1:T(8,128)(2,1)}, bf16[1280,2,64]{0,2,1:T(8,128)(2,1)S(1)}, u32[]{:S(2)}) copy-start(bf16[1280,2,64]{0,2,1:T(8,128)(2,1)S(1)} %get-tuple-element.55) | copy-start | bytes 983044
  250.3 29.4 %copy-start.15 = (bf16[1280,2,64]{0,2,1:T(8,128)(2,1)}, bf16[1280,2,64]{0,2,1:T(8,128)(2,1)S(1)}, u32[]{:S(2)}) copy-start(bf16[1280,2,64]{0,2,1:T(8,128)(2,1)S(1)} %get-tuple-element.59) | copy-start | bytes 983044
  250.3 29.5 %copy-start.24 = (bf16[1280,2,64]{0,2,1:T(8,128)(2,1)}, bf16[1280,2,64]{0,2,1:T(8,128)(2,1)S(1)}, u32[]{:S(2)}) copy-start(bf16[1280,2,64]{0,2,1:T(8,128)(2,1)S(1)} %get-tuple-element.56) | copy-start | bytes 983044
  253.2 6.3 collective-permute-start.3
  254.5 6.6 %collective-permute-start.2 = (bf16[320,64]{1,0:T(8,128)(2,1)S(1)}, bf16[320,64]{1,0:T(8,128)(2,1)S(1)}, u32[]{:S(2)}, u32[]{:S(2)}) collective-permute-start(bf16[320,64]{1,0:T(8,128)(2,1)S(1)} %get-tuple-element.40), channel_id=1, source_target_pairs={{0,8},{4,12},{1,9},{5,13},{2,10},{6,14},{3,11},{7,15},{16,24},{20,... | collective-permute-start | bytes 122888 | tf_op jit(solution)/shard_map/ppermute | solution.py:20
  294.8 21.0 %copy-start.20 = (bf16[1280,2,64]{0,2,1:T(8,128)(2,1)S(1)}, bf16[1280,2,64]{0,2,1:T(8,128)(2,1)}, u32[]{:S(2)}) copy-start(bf16[1280,2,64]{0,2,1:T(8,128)(2,1)} %copy-done.19) | copy-start | bytes 983044
  294.8 22.3 %copy-start.12 = (bf16[1280,2,64]{0,2,1:T(8,128)(2,1)S(1)}, bf16[1280,2,64]{0,2,1:T(8,128)(2,1)}, u32[]{:S(2)}) copy-start(bf16[1280,2,64]{0,2,1:T(8,128)(2,1)} %copy-done.11) | copy-start | bytes 983044
  294.8 23.6 %copy-start.16 = (bf16[1280,2,64]{0,2,1:T(8,128)(2,1)S(1)}, bf16[1280,2,64]{0,2,1:T(8,128)(2,1)}, u32[]{:S(2)}) copy-start(bf16[1280,2,64]{0,2,1:T(8,128)(2,1)} %copy-done.15) | copy-start | bytes 983044
  294.8 24.9 %copy-start.6 = (bf16[1280,2,64]{0,2,1:T(8,128)(2,1)S(1)}, bf16[1280,2,64]{0,2,1:T(8,128)(2,1)}, u32[]{:S(2)}) copy-start(bf16[1280,2,64]{0,2,1:T(8,128)(2,1)} %copy-done.5) | copy-start | bytes 983044
  294.8 26.1 %copy-start.10 = (bf16[1280,2,64]{0,2,1:T(8,128)(2,1)S(1)}, bf16[1280,2,64]{0,2,1:T(8,128)(2,1)}, u32[]{:S(2)}) copy-start(bf16[1280,2,64]{0,2,1:T(8,128)(2,1)} %copy-done.9) | copy-start | bytes 983044
  294.8 27.4 %copy-start.14 = (bf16[1280,2,64]{0,2,1:T(8,128)(2,1)S(1)}, bf16[1280,2,64]{0,2,1:T(8,128)(2,1)}, u32[]{:S(2)}) copy-start(bf16[1280,2,64]{0,2,1:T(8,128)(2,1)} %copy-done.13) | copy-start | bytes 983044
  294.8 332.8 %reduce-scatter.7.cloned.1.call-start = ((), (), s32[]{:S(2)}) async-start(), calls=%async_computation.4 | async-start | bytes 9420800
  315.8 7.7 %copy-start.4 = (bf16[1280,2,64]{0,2,1:T(8,128)(2,1)S(1)}, bf16[1280,2,64]{0,2,1:T(8,128)(2,1)}, u32[]{:S(2)}) copy-start(bf16[1280,2,64]{0,2,1:T(8,128)(2,1)} %copy-done.3) | copy-start | bytes 983044
  315.8 9.0 %copy-start.8 = (bf16[1280,2,64]{0,2,1:T(8,128)(2,1)S(1)}, bf16[1280,2,64]{0,2,1:T(8,128)(2,1)}, u32[]{:S(2)}) copy-start(bf16[1280,2,64]{0,2,1:T(8,128)(2,1)} %copy-done.7) | copy-start | bytes 983044
  315.8 10.3 %copy-start.25 = (bf16[1280,2,64]{0,2,1:T(8,128)(2,1)S(1)}, bf16[1280,2,64]{0,2,1:T(8,128)(2,1)}, u32[]{:S(2)}) copy-start(bf16[1280,2,64]{0,2,1:T(8,128)(2,1)} %copy-done.24) | copy-start | bytes 983044
  395.8 6.0 copy-start.17
  395.8 165.4 %all-to-all-start.1 = ((bf16[4,2,460800]{2,1,0:T(2,128)(2,1)}), bf16[4,2,460800]{2,1,0:T(2,128)(2,1)}, u32[]{:S(2)}, u32[]{:S(2)}) async-start(bf16[4,2,460800]{2,1,0:T(2,128)(2,1)} %reshape.125), calls=%async_computation.1 | async-start | bytes 14745600 | tf_op jit(solution)/shard_map/all_to_all | solution.py:92
  612.7 13.9 %copy-start.18 = (bf16[1280,2,64]{0,2,1:T(8,128)(2,1)S(1)}, bf16[1280,2,64]{0,2,1:T(8,128)(2,1)}, u32[]{:S(2)}) copy-start(bf16[1280,2,64]{0,2,1:T(8,128)(2,1)} %get-tuple-element.42) | copy-start | bytes 983044
  614.2 8.3 %copy-start.2 = (bf16[320,1280]{1,0:T(8,128)(2,1)S(1)}, bf16[320,1280]{1,0:T(8,128)(2,1)}, u32[]{:S(2)}) copy-start(bf16[320,1280]{1,0:T(8,128)(2,1)} %squeeze.92) | copy-start | bytes 2457604
  614.2 9.6 %copy-start.1 = (bf16[320,1280]{1,0:T(8,128)(2,1)S(1)}, bf16[320,1280]{1,0:T(8,128)(2,1)}, u32[]{:S(2)}) copy-start(bf16[320,1280]{1,0:T(8,128)(2,1)} %squeeze.93) | copy-start | bytes 2457604
Sparse Core Ops, SparseCore 0:
  294.9 35.7 reduce-scatter.8
  366.4 67.7 reduce-scatter.6
where the time goes:
time: 659 us; the launch traced here: 649 us
  local copies, waits for them, and re-layouts  243 us (37%)
  waiting for transfers between devices  160 us (24%)
  blocking collectives  154 us (23%)
  matrix products  37.1 us (6%)
  starting transfers between devices  29.3 us (4%)
  between operations  15 us (2%)
  other arithmetic  10.6 us (2%)
    unnamed x96, local copies, waits for them, and re-layouts  175 us
    all_gather x4, blocking collectives, circulate(): lax.all_gather(data, 'ch', axis=0, tiled=True)  154 us
    all_to_all x1, waiting for transfers between devices, on_device(): lax.all_to_all(jnp.transpose(spatial_weight, (0, 2, 1)), 'ch', split_axis...  153 us
    squeeze x10, local copies, waits for them, and re-layouts, contract(): weights[position]  21.6 us
    dot_general x20, matrix products, contract(): jnp.dot(weights[position], pieces[position], preferred_element_type=jnp.f...  19.3 us
    ppermute x8, starting transfers between devices, passed_along(): return lax.ppermute(shard, axis, pairs)  17 us
    slice x2, local copies, waits for them, and re-layouts, spatial_piece(): window = lax.slice_in_dim(padded, first_cell, first_cell + RT * W, axis=2)  13.8 us
  transfers between devices with their start and end apart: 12, of which 5 were waited for; matrix products, arithmetic and copies ran while one was open for 31% of the time, Pallas kernels for 0%

commit v1 on v0

--- a/solution.py
+++ b/solution.py
@@ -12,6 +12,12 @@
     ((row_step, col_step) for row_step in (-1, 0, 1) for col_step in (-1, 0, 1))
 )
 frame_offsets = (-1, 0, 1)
+
+
+def trade_parts(array, axis, split, join):
+    parts = jnp.split(array, lax.axis_size(axis), axis=split)
+    incoming = lax.all_to_all(jnp.stack(parts), axis, 0, 0)
+    return jnp.concatenate(incoming, axis=join)
 
 
 def passed_along(shard, axis, by):
@@ -89,9 +95,7 @@
     channels, tile_cells = latents.shape
     grad_scale = 1.0 / math.sqrt(tile_cells * lax.axis_size("st"))
     spatial_back, temporal_back = (
-        lax.all_to_all(
-            jnp.transpose(spatial_weight, (0, 2, 1)), "ch", split_axis=1, concat_axis=2, tiled=True
-        ),
+        trade_parts(jnp.transpose(spatial_weight, (0, 2, 1)), "ch", 1, 2),
         lax.all_to_all(
             jnp.transpose(temporal_weight, (0, 2, 1)), "ch", split_axis=1, concat_axis=2, tiled=True
         ),

time: 659 us -> 588 us (0.89); the launches traced: 649 us -> 586 us
  local copies, waits for them, and re-layouts: 243 us -> 149 us
  waiting for transfers between devices: 160 us -> 192 us
  matrix products: 37.1 us -> 30.3 us
    unnamed x96 -> x100, local copies, waits for them, and re-layouts: 175 us -> 109 us
    all_to_all x1, waiting for transfers between devices: 153 us -> 185 us  [trade_parts(): incoming = lax.all_to_all(jnp.stack(parts), axis, 0, 0)]
    squeeze x10 -> x2, local copies, waits for them, and re-layouts: 21.6 us -> 4.41 us  [contract(): weights[position]]
    all_to_all x1 -> x0, local copies, waits for them, and re-layouts: 12.7 us -> none  [on_device(): lax.all_to_all(jnp.transpose(spatial_weight, (0, 2, 1)), 'ch', split_axis...]
    dot_general x20, matrix products: 19.3 us -> 11.8 us  [contract(): jnp.dot(weights[position], pieces[position], preferred_element_type=jnp.f...]
  transfers between devices with their start and end apart: 12 -> 12, of which waited for: 5 -> 5; matrix products, arithmetic and copies ran while one was open for 31% -> 18% of each run, Pallas kernels for 0% -> 0%
where the time goes in v1:
time: 588 us; the launch traced here: 586 us
  waiting for transfers between devices  192 us (33%)
  blocking collectives  154 us (26%)
  local copies, waits for them, and re-layouts  149 us (25%)
  matrix products  30.3 us (5%)
  starting transfers between devices  29.8 us (5%)
  other arithmetic  16 us (3%)
  between operations  14.8 us (3%)
    all_to_all x1, waiting for transfers between devices, trade_parts(): incoming = lax.all_to_all(jnp.stack(parts), axis, 0, 0)  185 us
    all_gather x4, blocking collectives, circulate(): lax.all_gather(data, 'ch', axis=0, tiled=True)  154 us
    unnamed x100, local copies, waits for them, and re-layouts  109 us
    ppermute x8, starting transfers between devices, passed_along(): return lax.ppermute(shard, axis, pairs)  17 us
    dot_general x12, matrix products, outer_sums(): lax.dot_general(gradient, tap_piece, contraction, preferred_element_type=...  14.6 us
    slice x2, local copies, waits for them, and re-layouts, spatial_piece(): window = lax.slice_in_dim(padded, first_cell, first_cell + RT * W, axis=2)  13.8 us
    dot_general x20, matrix products, contract(): jnp.dot(weights[position], pieces[position], preferred_element_type=jnp.f...  11.8 us
  transfers between devices with their start and end apart: 12, of which 5 were waited for; matrix products, arithmetic and copies ran while one was open for 18% of the time, Pallas kernels for 0%

profile of v1, /device:TPU:0, one launch (start us, length us, event | category | flops | bytes accessed | tf_op | source)
XLA Modules:
  0.0 585.9 jit_solution(3409529734730644308)
XLA Ops:
  7.2 7.7 %copy.22 = bf16[3,320,1280]{1,0,2:T(4,128)(2,1)} copy(bf16[3,320,1280]{2,1,0:T(8,128)(2,1)} %param.6) | data formatting | bytes 4915200 | tf_op args[2]
  14.9 6.3 %all-to-all-start = ((bf16[3,1280,320]{2,0,1:T(4,128)(2,1)}), bf16[3,1280,320]{2,0,1:T(4,128)(2,1)}, u32[]{:S(2)}, u32[]{:S(2)}) async-start(bf16[3,1280,320]{2,0,1:T(4,128)(2,1)} %bitcast.205), calls=%async_computation | async-start | bytes 7864320 | tf_op jit(solution)/shard_map/all_to_all | solution.py:99
  21.3 1.3 collective-permute-start.5
  22.6 4.6 collective-permute-start.4
  27.3 1.3 collective-permute-start
  28.6 1.3 collective-permute-start.1
  30.0 1.7 collective-permute-done.1
  33.0 87.4 %all_gather.16 = bf16[1280,256]{1,0:T(8,128)(2,1)S(1)} all-gather(bf16[320,256]{1,0:T(8,128)(2,1)S(1)} %pad_maximum_fusion.3), channel_id=1, replica_groups=mesh['groups'=2,'st'=4,'ch'=4] {'ch'}, dimensions={0}, use_global_device_ids=true | all-gather | bytes 819200 | tf_op jit(solution)/shard_map/all_gather | solution.py:34
  120.4 24.1 %all_gather.14 = bf16[1280,2,130]{2,1,0:T(2,128)(2,1)S(1)} all-gather(bf16[320,2,130]{2,1,0:T(2,128)(2,1)S(1)} %copy.12), channel_id=1, replica_groups=mesh['groups'=2,'st'=4,'ch'=4] {'ch'}, dimensions={0}, use_global_device_ids=true | all-gather | bytes 832000 | tf_op jit(solution)/shard_map/all_gather | solution.py:34
  144.4 4.9 copy.58
  149.3 2.3 fusion.69
  151.6 2.8 squeeze.85
  154.4 2.8 squeeze.84
  157.1 1.7 squeeze.86
  158.8 1.6 fusion.59
  160.4 1.5 convolution_add_fusion.1
  161.9 1.5 fusion.29
  163.6 1.5 collective-permute-start.6
  165.1 6.9 %fusion.71 = (bf16[1280,2,64]{2,1,0:T(2,128)(2,1)S(1)}, bf16[1280,2,64]{2,1,0:T(2,128)(2,1)}, bf16[1280,2,64]{2,1,0:T(2,128)(2,1)}, bf16[1280,2,64]{2,1,0:T(2,12...) fusion(bf16[1280,2,130]{2,1,0:T(2,128)(2,1)S(1)} %all_gather.14), kind=kLoop, calls=%fused_computation.140 | loop fusion | bytes 5898240 | tf_op jit(solution)/shard_map/slice | solution.py:55
  172.0 2.0 copy.42
  174.0 2.0 copy.45
  176.1 2.0 copy.39
  178.1 2.0 copy.43
  180.1 2.0 copy.46
  182.1 2.0 copy.40
  184.1 2.0 copy.44
  188.4 1.3 collective-permute-start.7
  189.7 3.7 collective-permute-done.7
  194.5 24.4 %all_gather.17 = bf16[1280,2,130]{2,1,0:T(2,128)(2,1)S(1)} all-gather(bf16[320,2,130]{2,1,0:T(2,128)(2,1)S(1)} %copy.25), channel_id=1, replica_groups=mesh['groups'=2,'st'=4,'ch'=4] {'ch'}, dimensions={0}, use_global_device_ids=true | all-gather | bytes 832000 | tf_op jit(solution)/shard_map/all_gather | solution.py:34
  218.9 6.9 %fusion.70 = (bf16[1280,2,64]{2,1,0:T(2,128)(2,1)S(1)}, bf16[1280,2,64]{2,1,0:T(2,128)(2,1)}, bf16[1280,2,64]{2,1,0:T(2,128)(2,1)}, bf16[1280,2,64]{2,1,0:T(2,12...) fusion(bf16[1280,2,130]{2,1,0:T(2,128)(2,1)S(1)} %all_gather.17), kind=kLoop, calls=%fused_computation.139 | loop fusion | bytes 5898240 | tf_op jit(solution)/shard_map/slice | solution.py:55
  229.1 2.2 copy.55
  231.3 2.0 copy.49
  233.3 2.0 copy.52
  235.3 2.0 copy.54
  237.3 2.0 copy.48
  239.3 2.0 copy.51
  241.4 2.7 broadcast_select_fusion.12
  244.8 1.5 fusion.44
  246.3 2.5 broadcast_select_fusion.6
  253.2 1.3 collective-permute-start.3
  254.5 4.6 collective-permute-start.2
  259.5 1.6 collective-permute-done.2
  261.3 17.7 %all_gather.15 = bf16[1280,256]{1,0:T(8,128)(2,1)S(1)} all-gather(bf16[320,256]{1,0:T(8,128)(2,1)S(1)} %pad_maximum_fusion.2), channel_id=1, replica_groups=mesh['groups'=2,'st'=4,'ch'=4] {'ch'}, dimensions={0}, use_global_device_ids=true | all-gather | bytes 819200 | tf_op jit(solution)/shard_map/all_gather | solution.py:34
  280.5 6.0 %copy.37 = bf16[3,320,1280]{1,0,2:T(4,128)(2,1)} copy(bf16[3,320,1280]{2,1,0:T(8,128)(2,1)S(1)} %pad_maximum_fusion.1) | data formatting | bytes 4915200
  286.6 8.4 %reshape.128 = bf16[1280,960]{1,0:T(8,128)(2,1)} reshape(bf16[1280,3,320]{2,1,0:T(4,128)(2,1)} %bitcast.206) | data formatting | bytes 4915200
  295.1 2.2 fusion.1
  297.3 1.3 fusion.3
  298.6 1.3 fusion.5
  299.8 1.3 fusion.7
  301.1 1.3 fusion.9
  302.4 1.3 fusion.11
  303.7 1.3 fusion.13
  306.2 2.3 fusion.17
  308.5 20.1 %copy.35 = bf16[9,320,1280]{1,0,2:T(8,128)(2,1)} copy(bf16[9,320,1280]{2,1,0:T(8,128)(2,1)} %fusion.17) | data formatting | bytes 14745600
  328.6 18.8 %reshape.126 = bf16[1280,2880]{1,0:T(8,128)(2,1)} reshape(bf16[1280,9,320]{2,1,0:T(8,128)(2,1)} %bitcast.201) | data formatting | bytes 14745600
  347.4 5.3 slice_bitcast_fusion.3
  352.8 5.4 pad_maximum_fusion
  358.1 6.4 %all-to-all-start.1 = ((bf16[4,9,320,320]{2,3,1,0:T(8,128)(2,1)}), bf16[4,9,320,320]{2,3,1,0:T(8,128)(2,1)}, u32[]{:S(2)}, u32[]{:S(2)}) async-start(bf16[4,9,320,320]{2,3,1,0:T(8,128)(2,1)} %pad_maximum_fusion), calls=%async_computation.1 | async-start | bytes 17694720 | tf_op jit(solution)/shard_map/all_to_all | solution.py:19
  366.4 2.4 reshape.129
  371.3 184.6 %all-to-all-done.1 = bf16[4,9,320,320]{2,3,1,0:T(8,128)(2,1)} async-done(((bf16[4,9,320,320]{2,3,1,0:T(8,128)(2,1)}), bf16[4,9,320,320]{2,3,1,0:T(8,128)(2,1)}, u32[]{:S(2)}, u32[]{:S(2)}) %all-to-all-start.1) | async-done | bytes 7372832 | tf_op jit(solution)/shard_map/all_to_all | solution.py:19
  555.9 4.3 fusion.68
  565.0 5.6 reshape.127
  570.6 6.0 %copy.36 = bf16[9,320,320]{2,1,0:T(8,128)(2,1)S(1)} copy(bf16[9,320,320]{1,0,2:T(8,128)(2,1)} %bitcast.207) | data formatting | bytes 3686400
  576.6 2.5 convert_multiply_fusion
  (138 shorter events, 25.6 us)
Async XLA Ops:
  7.2 14.0 %copy-start = (bf16[320,128]{1,0:T(8,128)(2,1)S(1)}, bf16[320,128]{1,0:T(8,128)(2,1)}, u32[]{:S(2)}) copy-start(bf16[320,128]{1,0:T(8,128)(2,1)} %param.7) | copy-start | bytes 245764
  7.2 20.0 %copy-start.33 = (bf16[320,128]{1,0:T(8,128)(2,1)S(1)}, bf16[320,128]{1,0:T(8,128)(2,1)}, u32[]{:S(2)}) copy-start(bf16[320,128]{1,0:T(8,128)(2,1)} %param.4) | copy-start | bytes 245764
  14.9 129.6 %all-to-all-start = ((bf16[3,1280,320]{2,0,1:T(4,128)(2,1)}), bf16[3,1280,320]{2,0,1:T(4,128)(2,1)}, u32[]{:S(2)}, u32[]{:S(2)}) async-start(bf16[3,1280,320]{2,0,1:T(4,128)(2,1)} %bitcast.205), calls=%async_computation | async-start | bytes 7864320 | tf_op jit(solution)/shard_map/all_to_all | solution.py:99
  21.2 345.2 %reduce-scatter.9.cloned.1.call-start = ((), (), s32[]{:S(2)}) async-start(), calls=%async_computation.5 | async-start | bytes 3276800
  21.3 11.5 %collective-permute-start.5 = (bf16[320,64]{1,0:T(8,128)(2,1)S(1)}, bf16[320,64]{1,0:T(8,128)(2,1)S(1)}, u32[]{:S(2)}, u32[]{:S(2)}) collective-permute-start(bf16[320,64]{1,0:T(8,128)(2,1)S(1)} %get-tuple-element.43), channel_id=1, source_target_pairs={{8,0},{12,4},{9,1},{13,5},{10,2},{14,6},{11,3},{15,7},{24,16},{28,... | collective-permute-start | bytes 122888 | tf_op jit(solution)/shard_map/ppermute | solution.py:26
  22.6 10.2 %collective-permute-start.4 = (bf16[320,64]{1,0:T(8,128)(2,1)S(1)}, bf16[320,64]{1,0:T(8,128)(2,1)S(1)}, u32[]{:S(2)}, u32[]{:S(2)}) collective-permute-start(bf16[320,64]{1,0:T(8,128)(2,1)S(1)} %get-tuple-element.42), channel_id=1, source_target_pairs={{0,8},{4,12},{1,9},{5,13},{2,10},{6,14},{3,11},{7,15},{16,24},{20,... | collective-permute-start | bytes 122888 | tf_op jit(solution)/shard_map/ppermute | solution.py:26
  27.3 2.7 collective-permute-start
  28.6 3.1 collective-permute-start.1
  163.6 26.0 %collective-permute-start.6 = (bf16[320,2,32]{0,2,1:T(8,128)(2,1)S(1)}, bf16[320,2,32]{0,2,1:T(8,128)(2,1)S(1)}, u32[]{:S(2)}, u32[]{:S(2)}) collective-permute-start(bf16[320,2,32]{0,2,1:T(8,128)(2,1)S(1)} %get-tuple-element.39), channel_id=1, source_target_pairs={{0,4},{4,8},{8,12},{1,5},{5,9},{9,13},{2,6},{6,10},{10,14},{3,7},{... | collective-permute-start | bytes 122888 | tf_op jit(solution)/shard_map/ppermute | solution.py:26
  188.4 5.0 collective-permute-start.7
  229.1 19.8 %slice-start = ((s8[7372800]{0:T(1024)(128)(4,1)}), s8[3178496]{0:T(1024)(128)(4,1)S(1)}, s32[]{:S(2)}) async-start(s8[7372800]{0:T(1024)(128)(4,1)} %bitcast.203), calls=%async_computation.6 | async-start | bytes 6356992
  241.3 7.5 %slice-start.1 = ((s8[7372800]{0:T(1024)(128)(4,1)}), s8[4194304]{0:T(1024)(128)(4,1)S(1)}, s32[]{:S(2)}) async-start(s8[7372800]{0:T(1024)(128)(4,1)} %bitcast.203), calls=%async_computation.7 | async-start | bytes 8388608
  241.3 7.9 %copy-start.26 = (bf16[1280,2,64]{0,2,1:T(8,128)(2,1)S(1)}, bf16[1280,2,64]{0,2,1:T(8,128)(2,1)}, u32[]{:S(2)}) copy-start(bf16[1280,2,64]{0,2,1:T(8,128)(2,1)} %copy.44) | copy-start | bytes 983044
  241.3 7.9 %copy-start.27 = (bf16[1280,2,64]{0,2,1:T(8,128)(2,1)S(1)}, bf16[1280,2,64]{0,2,1:T(8,128)(2,1)}, u32[]{:S(2)}) copy-start(bf16[1280,2,64]{0,2,1:T(8,128)(2,1)} %copy.47) | copy-start | bytes 983044
  241.3 7.9 %copy-start.28 = (bf16[1280,2,64]{0,2,1:T(8,128)(2,1)S(1)}, bf16[1280,2,64]{0,2,1:T(8,128)(2,1)}, u32[]{:S(2)}) copy-start(bf16[1280,2,64]{0,2,1:T(8,128)(2,1)} %copy.41) | copy-start | bytes 983044
  241.3 8.0 %copy-start.30 = (bf16[1280,2,64]{0,2,1:T(8,128)(2,1)S(1)}, bf16[1280,2,64]{0,2,1:T(8,128)(2,1)}, u32[]{:S(2)}) copy-start(bf16[1280,2,64]{0,2,1:T(8,128)(2,1)} %copy.54) | copy-start | bytes 983044
  241.3 8.0 %copy-start.31 = (bf16[1280,2,64]{0,2,1:T(8,128)(2,1)S(1)}, bf16[1280,2,64]{0,2,1:T(8,128)(2,1)}, u32[]{:S(2)}) copy-start(bf16[1280,2,64]{0,2,1:T(8,128)(2,1)} %copy.48) | copy-start | bytes 983044
  241.4 8.0 %copy-start.32 = (bf16[1280,2,64]{0,2,1:T(8,128)(2,1)S(1)}, bf16[1280,2,64]{0,2,1:T(8,128)(2,1)}, u32[]{:S(2)}) copy-start(bf16[1280,2,64]{0,2,1:T(8,128)(2,1)} %copy.51) | copy-start | bytes 983044
  244.1 0.7 copy-start.25
  244.1 7.5 %copy-start.3 = (bf16[1280,2,64]{0,2,1:T(8,128)(2,1)}, bf16[1280,2,64]{0,2,1:T(8,128)(2,1)S(1)}, u32[]{:S(2)}) copy-start(bf16[1280,2,64]{0,2,1:T(8,128)(2,1)S(1)} %get-tuple-element.47) | copy-start | bytes 983044
  244.1 7.9 %copy-start.1 = (bf16[1280,2,64]{0,2,1:T(8,128)(2,1)}, bf16[1280,2,64]{0,2,1:T(8,128)(2,1)S(1)}, u32[]{:S(2)}) copy-start(bf16[1280,2,64]{0,2,1:T(8,128)(2,1)S(1)} %get-tuple-element.48) | copy-start | bytes 983044
  248.8 4.3 copy-start.5
  248.8 4.3 copy-start.7
  248.8 4.3 copy-start.9
  250.4 29.4 %copy-start.11 = (bf16[1280,2,64]{0,2,1:T(8,128)(2,1)}, bf16[1280,2,64]{0,2,1:T(8,128)(2,1)S(1)}, u32[]{:S(2)}) copy-start(bf16[1280,2,64]{0,2,1:T(8,128)(2,1)S(1)} %get-tuple-element.59) | copy-start | bytes 983044
  250.4 29.4 %copy-start.13 = (bf16[1280,2,64]{0,2,1:T(8,128)(2,1)}, bf16[1280,2,64]{0,2,1:T(8,128)(2,1)S(1)}, u32[]{:S(2)}) copy-start(bf16[1280,2,64]{0,2,1:T(8,128)(2,1)S(1)} %get-tuple-element.63) | copy-start | bytes 983044
  250.4 29.4 %copy-start.29 = (bf16[1280,2,64]{0,2,1:T(8,128)(2,1)}, bf16[1280,2,64]{0,2,1:T(8,128)(2,1)S(1)}, u32[]{:S(2)}) copy-start(bf16[1280,2,64]{0,2,1:T(8,128)(2,1)S(1)} %get-tuple-element.60) | copy-start | bytes 983044
  253.2 6.3 %collective-permute-start.3 = (bf16[320,64]{1,0:T(8,128)(2,1)S(1)}, bf16[320,64]{1,0:T(8,128)(2,1)S(1)}, u32[]{:S(2)}, u32[]{:S(2)}) collective-permute-start(bf16[320,64]{1,0:T(8,128)(2,1)S(1)} %get-tuple-element.45), channel_id=1, source_target_pairs={{8,0},{12,4},{9,1},{13,5},{10,2},{14,6},{11,3},{15,7},{24,16},{28,... | collective-permute-start | bytes 122888 | tf_op jit(solution)/shard_map/ppermute | solution.py:26
  254.5 6.6 %collective-permute-start.2 = (bf16[320,64]{1,0:T(8,128)(2,1)S(1)}, bf16[320,64]{1,0:T(8,128)(2,1)S(1)}, u32[]{:S(2)}, u32[]{:S(2)}) collective-permute-start(bf16[320,64]{1,0:T(8,128)(2,1)S(1)} %get-tuple-element.44), channel_id=1, source_target_pairs={{0,8},{4,12},{1,9},{5,13},{2,10},{6,14},{3,11},{7,15},{16,24},{20,... | collective-permute-start | bytes 122888 | tf_op jit(solution)/shard_map/ppermute | solution.py:26
  286.5 10.8 %copy-start.10 = (bf16[1280,2,64]{0,2,1:T(8,128)(2,1)S(1)}, bf16[1280,2,64]{0,2,1:T(8,128)(2,1)}, u32[]{:S(2)}) copy-start(bf16[1280,2,64]{0,2,1:T(8,128)(2,1)} %copy-done.9) | copy-start | bytes 983044
  286.5 12.0 %copy-start.14 = (bf16[1280,2,64]{0,2,1:T(8,128)(2,1)S(1)}, bf16[1280,2,64]{0,2,1:T(8,128)(2,1)}, u32[]{:S(2)}) copy-start(bf16[1280,2,64]{0,2,1:T(8,128)(2,1)} %copy-done.13) | copy-start | bytes 983044
  286.5 13.3 %copy-start.4 = (bf16[1280,2,64]{0,2,1:T(8,128)(2,1)S(1)}, bf16[1280,2,64]{0,2,1:T(8,128)(2,1)}, u32[]{:S(2)}) copy-start(bf16[1280,2,64]{0,2,1:T(8,128)(2,1)} %copy-done.3) | copy-start | bytes 983044
  286.5 14.6 %copy-start.8 = (bf16[1280,2,64]{0,2,1:T(8,128)(2,1)S(1)}, bf16[1280,2,64]{0,2,1:T(8,128)(2,1)}, u32[]{:S(2)}) copy-start(bf16[1280,2,64]{0,2,1:T(8,128)(2,1)} %copy-done.7) | copy-start | bytes 983044
  286.5 15.9 %copy-start.12 = (bf16[1280,2,64]{0,2,1:T(8,128)(2,1)S(1)}, bf16[1280,2,64]{0,2,1:T(8,128)(2,1)}, u32[]{:S(2)}) copy-start(bf16[1280,2,64]{0,2,1:T(8,128)(2,1)} %copy-done.11) | copy-start | bytes 983044
  286.5 17.1 %copy-start.2 = (bf16[1280,2,64]{0,2,1:T(8,128)(2,1)S(1)}, bf16[1280,2,64]{0,2,1:T(8,128)(2,1)}, u32[]{:S(2)}) copy-start(bf16[1280,2,64]{0,2,1:T(8,128)(2,1)} %copy-done.1) | copy-start | bytes 983044
  286.6 18.4 %copy-start.6 = (bf16[1280,2,64]{0,2,1:T(8,128)(2,1)S(1)}, bf16[1280,2,64]{0,2,1:T(8,128)(2,1)}, u32[]{:S(2)}) copy-start(bf16[1280,2,64]{0,2,1:T(8,128)(2,1)} %copy-done.5) | copy-start | bytes 983044
  295.0 270.0 %reduce-scatter.7.cloned.1.call-start = ((), (), s32[]{:S(2)}) async-start(), calls=%async_computation.4 | async-start | bytes 9420800
  358.1 6.4 %copy-start.15 = (bf16[3,320,1280]{2,1,0:T(8,128)(2,1)S(1)}, bf16[3,320,1280]{2,1,0:T(8,128)(2,1)}, u32[]{:S(2)}) copy-start(bf16[3,320,1280]{2,1,0:T(8,128)(2,1)} %param.6) | copy-start | bytes 7372804
  358.1 197.8 %all-to-all-start.1 = ((bf16[4,9,320,320]{2,3,1,0:T(8,128)(2,1)}), bf16[4,9,320,320]{2,3,1,0:T(8,128)(2,1)}, u32[]{:S(2)}, u32[]{:S(2)}) async-start(bf16[4,9,320,320]{2,3,1,0:T(8,128)(2,1)} %pad_maximum_fusion), calls=%async_computation.1 | async-start | bytes 17694720 | tf_op jit(solution)/shard_map/all_to_all | solution.py:19
  555.9 4.4 copy-start.24
  555.9 4.8 copy-start.22
  555.9 5.3 copy-start.19
  555.9 5.7 copy-start.23
  555.9 6.2 %copy-start.20 = (bf16[1280,2,64]{0,2,1:T(8,128)(2,1)S(1)}, bf16[1280,2,64]{0,2,1:T(8,128)(2,1)}, u32[]{:S(2)}) copy-start(bf16[1280,2,64]{0,2,1:T(8,128)(2,1)} %get-tuple-element.56) | copy-start | bytes 983044
  560.3 2.3 copy-start.17
  560.3 2.8 copy-start.21
  560.3 3.2 copy-start.18
  560.3 3.7 copy-start.16
Sparse Core Ops, SparseCore 0:
  295.1 35.8 reduce-scatter.8
  347.5 67.9 reduce-scatter.6
